TPU v7x, 32 devices: a whole 2x2x4 slice. The times are simulated.
32 devices in a mesh: row: 4 (over y, x), col: 8 (over z, core).
Axes of the slice: x: 2, y: 2, z: 4, core: 2. Of those that a mesh axis runs over, the one named last changes fastest.
Arguments:
- parent_front: bfloat16 [28672, 28672], P('row', 'col'), may hold values from -6 to 6
- child_update: bfloat16 [2, 14336, 14336], P(None, 'row', 'col'), may hold values from -6 to 6
- parent_test: bfloat16 [28672, 448], P('col'), may hold values from -0.03125 to 0.03125
- child_test: bfloat16 [2, 14336, 448], P(None, 'col'), may hold values from -0.046875 to 0.046875
- child_map: int32 [2, 112], replicated, may hold values from 0 to 223, as said below
Outputs:
- leaf_basis: bfloat16 [224, 128, 448], P('row', 'col')
- couplings: float32 [32, 448, 448], P('row', 'col')
Inputs may be any that keep to these rules, and one draw needn't show every extreme that they name: `child_map`: for each child the entries rise strictly along its blocks, and entry j is at least j.
All inputs are finite; a program needn't handle non-finite values.
Results may differ from a plain program's by a relative error of at most 0.006.
Values may be sent and summed in bfloat16 or wider, within the bound.
A program may use at most 192 MiB of HBM per device.

v0:
```python
import math

import jax
import jax.numpy as jnp
from jax import lax
from jax.sharding import PartitionSpec as P

LEAF = 896
BLOCK = 128


HIGH = lax.Precision.HIGHEST


def spread(block, axis, holder):
    block = jnp.where(lax.axis_index(axis) == holder, block, jnp.zeros_like(block))
    return lax.psum(block, axis)


def finish(leaves, gram_matrix):
    factor = jnp.linalg.cholesky(gram_matrix)
    solved = lax.linalg.triangular_solve(
        factor, leaves, left_side=False, lower=True, transpose_a=True
    )
    return (solved * math.sqrt(LEAF)).astype(jnp.bfloat16)


def local(parent_front, child_update, parent_test, child_test, child_map):
    row_count = lax.axis_size("row")
    col_count = lax.axis_size("col")
    row_index = lax.axis_index("row")
    col_index = lax.axis_index("col")
    slab_rows = BLOCK // col_count
    own_blocks = parent_front.shape[0] // BLOCK
    kid_blocks = child_update.shape[1] // BLOCK
    probes = parent_test.shape[1]
    own_probe = jnp.dot(parent_front, parent_test, preferred_element_type=jnp.float32)
    own_probe = own_probe.reshape(own_blocks, BLOCK, probes)
    kid_probe = jnp.stack(
        [
            jnp.dot(child_update[which], child_test[which], preferred_element_type=jnp.float32)
            for which in range(2)
        ]
    )
    kid_probe = kid_probe.reshape(2, kid_blocks, BLOCK, probes)
    own_share, kid_share = (
        lax.psum_scatter(own_probe, "col", scatter_dimension=1, tiled=True),
        lax.psum_scatter(kid_probe, "col", scatter_dimension=2, tiled=True),
    )
    first_block = row_index * own_blocks
    targets = jnp.arange(own_blocks, dtype=jnp.int32)
    mapped = child_map - first_block
    onehot = (mapped[:, None, :] == targets[None, :, None]).astype(jnp.float32)
    sample = own_share + jnp.einsum(
        "cpn,cnsr->psr",
        onehot,
        lax.all_gather(kid_share, "row", axis=1, tiled=True),
        precision=HIGH,
    )
    per_leaf = LEAF // BLOCK
    leaf_count = own_blocks // per_leaf
    leaves = sample.reshape(leaf_count, per_leaf * slab_rows, probes)
    partial_gram = jnp.einsum("lkr,lks->lrs", leaves, leaves, precision=HIGH)
    gram_matrix = lax.psum(partial_gram, "col")
    leaf_basis = finish(leaves, gram_matrix).reshape(own_blocks, slab_rows, probes)
    whole_basis = lax.all_gather(leaf_basis, "col", axis=1, tiled=True)
    bases = whole_basis.reshape(leaf_count, LEAF, probes)
    col_leaves = parent_front.shape[1] // LEAF
    shrink = 1.0 / math.sqrt(LEAF)

    def sibling_product(position):
        leaf_index = col_index * col_leaves + position
        sibling = jnp.bitwise_xor(leaf_index, 1)
        row_start = leaf_index % leaf_count * LEAF
        col_start = (sibling - col_index * col_leaves) * LEAF
        front_tile = lax.dynamic_slice(parent_front, (row_start, col_start), (LEAF, LEAF))
        product = (
            jnp.dot(front_tile, bases[sibling % leaf_count], preferred_element_type=jnp.float32)
            * shrink
        )
        return product.astype(jnp.bfloat16)

    products = lax.map(sibling_product, jnp.arange(col_leaves, dtype=jnp.int32))
    owner_span = col_count // row_count
    core_rows = probes // col_count
    received = [
        spread(products, "col", row_index * owner_span + offset) for offset in range(owner_span)
    ]
    products_all = jnp.concatenate(received, axis=0)
    columns = lax.dynamic_slice_in_dim(bases, col_index * core_rows, core_rows, 2)
    couplings = (
        jnp.einsum("lkr,lks->lrs", columns, products_all, preferred_element_type=jnp.float32)
        * shrink
    )
    return (leaf_basis, couplings)


def solution(mesh):
    in_specs = (P("row", "col"), P(None, "row", "col"), P("col", None), P(None, "col", None), P())
    out_specs = (P("row", "col", None), P("row", "col", None))
    return jax.shard_map(local, mesh=mesh, in_specs=in_specs, out_specs=out_specs, check_vma=False)
```

profile of v0, /device:TPU:0, one launch (start us, length us, event | category | flops | bytes accessed | tf_op | source)
XLA Modules:
  0.0 1988.1 jit_solution(7997422557833170795)
XLA Ops:
  7.2 9.5 fusion.77
  16.7 10.5 convolution_bitcast_fusion.1
  27.2 10.6 convolution_bitcast_fusion.2
  37.8 10.9 pad_maximum_fusion
  48.7 21.7 %copy.91 = f32[2,28,128,448]{3,0,1,2:T(2,128)} copy(f32[2,28,128,448]{2,3,1,0:T(8,128)} %pad_maximum_fusion) | data formatting | bytes 25690112 | tf_op jit(solution)/shard_map/stack | solution.py:39
  72.3 295.1 %all-reduce.11.cloned.1.call-done = f32[2,28,128,448]{3,0,1,2:T(2,128)} async-done(((f32[2,28,128,448]{3,0,1,2:T(2,128)}), f32[2,28,128,448]{3,0,1,2:T(2,128)}) %all-reduce.11.cloned.1.call-update) | async-done | bytes 12845072
  367.4 2.1 constant_dynamic-slice_fusion.1
  369.5 2.3 copy.92
  372.0 30.3 %convolution_bitcast_fusion = f32[56,8,56,128]{3,1,2,0:T(8,128)} fusion(bf16[7168,3584]{1,0:T(8,128)(2,1)} %param.7, bf16[3584,448]{0,1:T(8,128)(2,1)S(1)} %copy-done), kind=kOutput, calls=%fused_computation.11 | convolution fusion | flops 23018340352 | bytes 67436544 | tf_op jit(solution)/shard_map/dot_general | solution.py:37
  402.3 12.2 copy.136
  414.6 16.4 copy.90
  431.7 19.2 all-gather.3.cloned.1.call-done
  450.9 151.3 %reduce-scatter.2.cloned.1.call-done = f32[56,16,448]{2,0,1:T(8,128)} async-done(((f32[56,128,448]{2,0,1:T(8,128)}), f32[56,16,448]{2,0,1:T(8,128)}) %reduce-scatter.2.cloned.1.call-update) | async-done | bytes 1605648 | tf_op jit(solution)/shard_map/reduce_scatter | solution.py:47
  602.2 10.3 bitcast_add_fusion.1
  612.6 1.1 copy.94
  613.6 8.1 fusion.78
  622.3 0.8 iota_compare_fusion
  623.3 152.8 %all-reduce.9.cloned.1.call-done = f32[8,448,448]{1,2,0:T(8,128)} async-done(((f32[8,448,448]{1,2,0:T(8,128)}), f32[8,448,448]{1,2,0:T(8,128)}) %all-reduce.9.cloned.1.call-update) | async-done | bytes 6422544 | tf_op jit(solution)/shard_map/psum | solution.py:64
  776.1 8.5 copy.97
  784.6 7.0 fusion.13
  791.6 2.9 copy-done.3
  794.6 93.8 %custom-call.34 = f32[8,128,128]{2,1,0:T(8,128)S(1)} custom-call(f32[8,128,128]{2,1,0:T(8,128)S(1)} %cholesky.281), custom_call_target="Cholesky" | custom-call | tf_op jit(solution)/shard_map/jit(cholesky)/cholesky | solution.py:21
  888.4 4.0 cholesky.236
  892.4 79.2 %custom-call.35 = f32[8,1,128,128]{2,3,1,0:T(8,128)} custom-call(f32[8,1,128,128]{3,2,1,0:T(8,128)S(1)} %select_bitcast_fusion.2), custom_call_target="InvertDiagBlocksLowerTriangular" | custom-call | tf_op jit(solution)/shard_map/jit(cholesky)/cholesky | solution.py:21
  971.7 3.9 constant_dynamic-update-slice_fusion.3
  975.5 2.7 convolution_subtract_fusion
  978.2 1.1 copy-done.4
  979.3 94.0 %custom-call.36 = f32[8,128,128]{2,1,0:T(8,128)S(1)} custom-call(f32[8,128,128]{2,1,0:T(8,128)S(1)} %cholesky.285), custom_call_target="Cholesky" | custom-call | tf_op jit(solution)/shard_map/jit(cholesky)/cholesky | solution.py:21
  1073.3 1.0 select_bitcast_fusion.1
  1074.3 79.2 %custom-call.37 = f32[8,1,128,128]{2,3,1,0:T(8,128)} custom-call(f32[8,1,128,128]{3,2,1,0:T(8,128)S(1)} %get-tuple-element.154), custom_call_target="InvertDiagBlocksLowerTriangular" | custom-call | tf_op jit(solution)/shard_map/jit(cholesky)/cholesky | solution.py:21
  1153.5 3.1 convolution_dynamic-update-slice_fusion
  1156.7 3.6 fusion.38
  1160.3 0.8 cholesky.290
  1161.1 95.4 %custom-call.38 = f32[8,128,128]{2,1,0:T(8,128)} custom-call(f32[8,128,128]{2,1,0:T(8,128)} %cholesky.290), custom_call_target="Cholesky" | custom-call | tf_op jit(solution)/shard_map/jit(cholesky)/cholesky | solution.py:21
  1256.5 2.4 select_reduce_fusion.1
  1258.9 79.4 %custom-call.39 = f32[8,1,128,128]{2,3,1,0:T(8,128)S(1)} custom-call(f32[8,1,128,128]{3,2,1,0:T(8,128)} %get-tuple-element.152), custom_call_target="InvertDiagBlocksLowerTriangular" | custom-call | tf_op jit(solution)/shard_map/jit(cholesky)/cholesky | solution.py:21
  1338.3 1.4 convolution_dynamic-update-slice_fusion.1
  1339.6 2.5 convolution_subtract_fusion.3
  1342.2 46.9 %custom-call.40 = f32[8,64,64]{2,1,0:T(8,128)S(1)} custom-call(f32[8,64,64]{2,1,0:T(8,128)S(1)} %convolution_subtract_fusion.3), custom_call_target="Cholesky" | custom-call | tf_op jit(solution)/shard_map/jit(cholesky)/cholesky | solution.py:21
  1389.1 0.8 select_reduce_fusion.3
  1390.2 4.3 select_select_fusion
  1394.6 2.9 copy-done.2
  1397.5 12.5 while.16
  1398.1 3.6 bitcast_dynamic-update-slice_fusion.3
  1402.3 3.6 bitcast_dynamic-update-slice_fusion.3
  1406.4 3.6 bitcast_dynamic-update-slice_fusion.3
  1410.3 3.0 pad_maximum_fusion.1
  1413.3 316.1 %custom-call.41 = f32[8,4,128,128]{2,3,1,0:T(8,128)} custom-call(f32[8,4,128,128]{3,2,1,0:T(8,128)} %pad_maximum_fusion.1), custom_call_target="InvertDiagBlocksLowerTriangular" | custom-call | tf_op jit(solution)/shard_map/triangular_solve | solution.py:22
  1729.3 1.8 fusion.60
  1731.2 2.3 convolution_subtract_fusion.2
  1734.1 2.3 convolution_subtract_fusion.1
  1737.0 3.1 fusion.41
  1740.2 0.9 fusion.67
  1741.1 1.1 fusion.20
  1742.3 73.5 %all-gather.5.cloned.1.call-done = bf16[56,128,448]{2,1,0:T(8,128)(2,1)} async-done(((bf16[56,16,448]{2,1,0:T(8,128)(2,1)}), bf16[56,128,448]{2,1,0:T(8,128)(2,1)}) %all-gather.5.cloned.1.call-update) | async-done | bytes 6422544 | tf_op jit(solution)/shard_map/all_gather | solution.py:66
  1815.9 17.0 while.15
  1816.1 0.6 dynamic_slice.47
  1817.5 2.8 fusion.100
  1821.6 2.8 fusion.100
  1825.8 2.9 fusion.100
  1830.0 2.8 fusion.100
  1832.9 3.2 broadcast_select_fusion.1
  1836.1 137.2 %all-reduce.13.cloned.1.call-done = (bf16[4,896,448]{1,2,0:T(8,128)(2,1)}, bf16[4,896,448]{1,2,0:T(8,128)(2,1)}) async-done(((bf16[4,896,448]{1,2,0:T(8,128)(2,1)}, bf16[4,896,448]{1,2,0:T(8,128)(2,1)}), (bf16[4,896,448]{1,2,0:T(8,128)(2,1)}, bf16[4,896,448]{1,2,0:T(8,128)(2,1)})) %all-reduce.13.cloned.1.call-update) | async-done | bytes 6422544 | tf_op jit(solution)/shard_map/psum | solution.py:17
  1973.3 7.4 fusion.52
  (66 shorter events, 8.8 us)
Async XLA Ops:
  7.2 364.9 %copy-start = (bf16[3584,448]{0,1:T(8,128)(2,1)S(1)}, bf16[3584,448]{0,1:T(8,128)(2,1)}, u32[]{:S(2)}) copy-start(bf16[3584,448]{0,1:T(8,128)(2,1)} %param.9) | copy-start | bytes 9633796
  7.2 360.2 %all-reduce.11.cloned.1.call-start = ((), (), s32[]{:S(2)}) async-start(), calls=%async_computation.5 | async-start | bytes 29360128
  70.4 0.7 copy-start.10
  70.4 380.5 %all-gather.3.cloned.1.call-start = ((), (), s32[]{:S(2)}) async-start(), calls=%async_computation.2 | async-start | bytes 9175040 | tf_op jit(solution)/shard_map/all_gather | solution.py:57
  371.8 230.4 %reduce-scatter.2.cloned.1.call-start = ((), (), s32[]{:S(2)}) async-start(), calls=%async_computation.1 | async-start | bytes 16515072 | tf_op jit(solution)/shard_map/reduce_scatter | solution.py:47
  431.0 0.7 copy-start.9
  431.0 345.1 %all-reduce.9.cloned.1.call-start = ((), (), s32[]{:S(2)}) async-start(), calls=%async_computation.3 | async-start | bytes 14680064 | tf_op jit(solution)/shard_map/psum | solution.py:64
  621.7 1194.1 %all-gather.5.cloned.1.call-start = ((), (), s32[]{:S(2)}) async-start(), calls=%async_computation.4 | async-start | bytes 8257536 | tf_op jit(solution)/shard_map/all_gather | solution.py:66
  791.6 2.9 copy-start.3
  888.4 4.0 copy-start.5
  978.2 1.1 copy-start.4
  1073.3 80.2 %copy-start.7 = (f32[8,128,128]{2,1,0:T(8,128)}, f32[8,128,128]{2,1,0:T(8,128)S(1)}, u32[]{:S(2)}) copy-start(f32[8,128,128]{2,1,0:T(8,128)S(1)} %custom-call.36) | copy-start | bytes 1572868
  1153.5 103.0 %copy-start.6 = (f32[8,128,128]{2,1,0:T(8,128)S(1)}, f32[8,128,128]{2,1,0:T(8,128)}, u32[]{:S(2)}) copy-start(f32[8,128,128]{2,1,0:T(8,128)} %copy-done.5) | copy-start | bytes 1572868
  1394.6 2.9 copy-start.2
  1729.3 4.1 copy-start.8
  1742.2 231.1 %all-reduce.13.cloned.1.call-start = ((), (), s32[]{:S(2)}) async-start(), calls=%async_computation.6 | async-start | bytes 12845056 | tf_op jit(solution)/shard_map/psum | solution.py:17
  1973.3 7.4 copy-start.1
Sparse Core Ops, SparseCore 0:
  70.5 296.7 all-reduce.10
  371.9 78.9 all-gather.2
  453.2 148.9 reduce-scatter.1
  621.9 154.2 all-reduce.8
  1742.4 73.4 all-gather.4
  1836.2 137.0 all-reduce.12
where the time goes:
time: 2000 us; the launch traced here: 1990 us
  other arithmetic  919 us (46%)
  waiting for transfers between devices  829 us (41%)
  matrix products  118 us (6%)
  local copies, waits for them, and re-layouts  102 us (5%)
    another operation x18, other arithmetic, finish(): factor = jnp.linalg.cholesky(gram_matrix)  573 us
    another operation x8, other arithmetic, finish(): lax.linalg.triangular_solve(factor, leaves, left_side=False, lower=True,...  324 us
    unnamed x7, waiting for transfers between devices  295 us
    psum x1, waiting for transfers between devices, local(): gram_matrix = lax.psum(partial_gram, 'col')  153 us
    reduce_scatter x1, waiting for transfers between devices, local(): lax.psum_scatter(own_probe, 'col', scatter_dimension=1, tiled=True)  151 us
    psum x1, waiting for transfers between devices, spread(): return lax.psum(block, axis)  137 us
    all_gather x1, waiting for transfers between devices, local(): whole_basis = lax.all_gather(leaf_basis, 'col', axis=1, tiled=True)  73.5 us
  transfers between devices with their start and end apart: 6, of which 6 were waited for; matrix products, arithmetic and copies ran while one was open for 3% of the time, Pallas kernels for 0%

commit v1 on v0

v1 whole, which is shorter than its diff:
```python
import functools
import math

import jax
import jax.numpy as jnp
from jax import lax
from jax.experimental import pallas as pl
from jax.experimental.pallas import tpu as pltpu
from jax.sharding import PartitionSpec as P

LEAF = 896
BLOCK = 128
PIVOTS = 64
GROUP = 4

HIGH = lax.Precision.HIGHEST


def dot(a, b, dims):
    return lax.dot_general(
        a, b, (dims, ((), ())), precision=HIGH, preferred_element_type=jnp.float32
    )


def inverse_factor(tile, nb):
    ridx = lax.broadcasted_iota(jnp.int32, tile.shape, 0)
    lane = lax.broadcasted_iota(jnp.int32, tile.shape, 1)
    for j in range(0, nb, GROUP):
        cols = [
            jnp.broadcast_to(tile[:, nb + j + k : nb + j + k + 1], tile.shape)
            for k in range(GROUP)
        ]
        rows = [tile[j + k : j + k + 1, :] for k in range(GROUP)]
        for k in range(GROUP):
            at = j + k
            factor = jnp.where(ridx > at, cols[k] * (1.0 / cols[k][at : at + 1, :]), 0.0)
            for m in range(k + 1, GROUP):
                cols[m] = cols[m] - factor * cols[m][at : at + 1, :]
                rows[m] = rows[m] - factor[j + m : j + m + 1, :] * rows[k]
            cols[k] = factor
        for k in range(GROUP):
            tile = tile - cols[k] * rows[k]
    pivots = jnp.sum(jnp.where(lane == ridx + nb, tile, 0.0), axis=1, keepdims=True)
    return tile[:, :nb] * lax.rsqrt(pivots)


def basis_kernel(scale, yt_ref, qt_ref, gram_ref, work_ref):
    nb = PIVOTS
    probes = yt_ref.shape[0]
    work_ref[...] = yt_ref[...]
    gram_ref[...] = dot(yt_ref[...], yt_ref[...], ((1,), (1,)))

    def step(index, carry):
        start = pl.multiple_of(index * nb, nb)
        panel = gram_ref[pl.ds(start, nb), :]
        source = lax.broadcasted_iota(jnp.int32, (probes, 2 * nb), 0)
        lane = lax.broadcasted_iota(jnp.int32, (probes, 2 * nb), 1)
        pick = jnp.where((lane >= nb) & (source == lane - nb + start), 1.0, 0.0)
        eye = jnp.where(
            lax.broadcasted_iota(jnp.int32, (nb, 2 * nb), 0)
            == lax.broadcasted_iota(jnp.int32, (nb, 2 * nb), 1),
            1.0,
            0.0,
        )
        inverse = inverse_factor(dot(panel, pick, ((1,), (0,))) + eye, nb)
        top = dot(inverse, panel, ((1,), (0,)))
        solved = dot(inverse, work_ref[pl.ds(start, nb), :], ((1,), (0,)))
        qt_ref[pl.ds(start, nb), :] = (solved * scale).astype(qt_ref.dtype)
        gram_ref[...] -= dot(top, top, ((0,), (0,)))
        work_ref[...] -= dot(top, solved, ((0,), (0,)))
        return carry

    lax.fori_loop(0, probes // nb, step, 0)


def leaf_basis_of(yt):
    probes, rows = yt.shape
    return pl.pallas_call(
        functools.partial(basis_kernel, math.sqrt(LEAF)),
        out_shape=jax.ShapeDtypeStruct((probes, rows), jnp.bfloat16),
        in_specs=[pl.BlockSpec(memory_space=pltpu.VMEM)],
        out_specs=pl.BlockSpec(memory_space=pltpu.VMEM),
        scratch_shapes=[
            pltpu.VMEM((probes, probes), jnp.float32),
            pltpu.VMEM((probes, rows), jnp.float32),
        ],
        compiler_params=pltpu.CompilerParams(vmem_limit_bytes=40 << 20),
        cost_estimate=pl.CostEstimate(
            flops=40 * probes * probes * rows,
            bytes_accessed=6 * probes * rows,
            transcendentals=0,
        ),
        name="leaf_basis",
    )(yt)


def reduce_slabs(partial, col_count, col_index):
    blocks = partial.shape[0] // BLOCK
    slab = BLOCK // col_count
    pairs = col_count // 2
    probes = partial.shape[1]
    pair_index = col_index // 2
    parity = col_index % 2
    view = partial.reshape(blocks, pairs, 2, slab, probes)
    swapped = lax.ppermute(
        lax.dynamic_index_in_dim(view, 1 - parity, 2, False),
        "col",
        [(c, c ^ 1) for c in range(col_count)],
    )
    kept = lax.dynamic_index_in_dim(view, parity, 2, False)

    def piece(pair):
        return lax.dynamic_index_in_dim(kept, pair, 1, False) + lax.dynamic_index_in_dim(
            swapped, pair, 1, False
        )

    total = piece(pair_index)
    for shift in range(1, pairs):
        sent = piece((pair_index + shift) % pairs).astype(jnp.bfloat16)
        came = lax.ppermute(
            sent, "col", [(c, (c + 2 * shift) % col_count) for c in range(col_count)]
        )
        total = total + came.astype(jnp.float32)
    return total


def local(parent_front, child_update, parent_test, child_test, child_map):
    row_count = lax.axis_size("row")
    col_count = lax.axis_size("col")
    row_index = lax.axis_index("row")
    col_index = lax.axis_index("col")
    slab = BLOCK // col_count
    own_blocks = parent_front.shape[0] // BLOCK
    kid_blocks = child_update.shape[1] // BLOCK
    probes = parent_test.shape[1]
    per_leaf = LEAF // BLOCK
    leaf_count = own_blocks // per_leaf
    col_leaves = parent_front.shape[1] // LEAF
    shrink = 1.0 / math.sqrt(LEAF)

    kid_probe = jnp.einsum(
        "cmk,ckr->cmr", child_update, child_test, preferred_element_type=jnp.float32
    )
    kid_share = reduce_slabs(
        kid_probe.reshape(2 * kid_blocks * BLOCK, probes), col_count, col_index
    ).reshape(2, kid_blocks, slab, probes)
    all_kids = lax.all_gather(kid_share, "row", axis=1, tiled=True)

    own_probe = jnp.dot(parent_front, parent_test, preferred_element_type=jnp.float32)
    own_share = reduce_slabs(own_probe, col_count, col_index)

    targets = jnp.arange(own_blocks, dtype=jnp.int32)
    mapped = child_map - row_index * own_blocks
    onehot = (mapped[:, None, :] == targets[None, :, None]).astype(jnp.float32)
    sample = own_share + jnp.einsum("cpn,cnsr->psr", onehot, all_kids, precision=HIGH)

    by_leaf = sample.reshape(leaf_count, per_leaf * slab, probes)
    by_leaf = jnp.pad(by_leaf, ((0, col_count - leaf_count), (0, 0), (0, 0)))
    leaf_rows = lax.all_to_all(by_leaf, "col", 0, 0, tiled=True).reshape(LEAF, probes)

    front = parent_front
    pieces = []
    for position in range(col_leaves):
        sibling = col_index * col_leaves + position
        row_start = jnp.bitwise_xor(sibling, 1) % leaf_count * LEAF
        tile = lax.dynamic_slice(front, (row_start, position * LEAF), (LEAF, LEAF))
        routes = []
        for row in range(row_count):
            for slot in range(leaf_count):
                other = (row * leaf_count + slot) ^ 1
                if other % col_leaves == position:
                    routes.append(
                        (row * col_count + other // col_leaves, row * col_count + slot)
                    )
        pieces.append(lax.ppermute(tile, ("row", "col"), routes))
    wanted = jnp.bitwise_xor(col_index, 1) % col_leaves
    front_tile = pieces[0]
    for position in range(1, col_leaves):
        front_tile = jnp.where(wanted == position, pieces[position], front_tile)

    basis_t = leaf_basis_of(leaf_rows.T)
    basis = basis_t.T
    slabs = lax.all_to_all(
        basis.reshape(col_count, per_leaf * slab, probes), "col", 0, 0, tiled=True
    )
    leaf_basis = slabs[:leaf_count].reshape(own_blocks, slab, probes)

    natural = (
        basis.reshape(col_count, per_leaf, slab, probes)
        .transpose(1, 0, 2, 3)
        .reshape(LEAF, probes)
    )
    sibling_basis = lax.ppermute(natural, "col", [(c, c ^ 1) for c in range(col_count)])
    product = jnp.dot(front_tile, sibling_basis, preferred_element_type=jnp.float32) * shrink
    core = (
        lax.dot_general(
            natural,
            product.astype(jnp.bfloat16),
            (((0,), (0,)), ((), ())),
            preferred_element_type=jnp.float32,
        )
        * shrink
    )
    cores = lax.all_to_all(
        core.reshape(col_count, probes // col_count, probes), "col", 0, 0, tiled=True
    )
    return (leaf_basis, cores[:leaf_count])


def solution(mesh):
    in_specs = (P("row", "col"), P(None, "row", "col"), P("col", None), P(None, "col", None), P())
    out_specs = (P("row", "col", None), P("row", "col", None))
    return jax.shard_map(local, mesh=mesh, in_specs=in_specs, out_specs=out_specs, check_vma=False)
```

time: 2000 us -> 514 us (0.26)
  other arithmetic: 919 us -> 18.6 us
  waiting for transfers between devices: 829 us -> 225 us
  starting transfers between devices: 1.04 us -> 79.9 us
  local copies, waits for them, and re-layouts: 102 us -> 50.8 us
  matrix products: 118 us -> 73.5 us
  Pallas kernels: 0 us -> 42.2 us
    another operation x28 -> x0, other arithmetic: 908 us -> none  [the longest x18 573 us: finish(): factor = jnp.linalg.cholesky(gram_matrix)]
    unnamed x7 -> x1, waiting for transfers between devices: 295 us -> 0.02 us
    psum x2 -> x0, waiting for transfers between devices: 290 us -> none  [the longest x1 153 us: local(): gram_matrix = lax.psum(partial_gram, 'col')]
    ppermute x0 -> x13, waiting for transfers between devices: none -> 171 us  [the longest x6 150 us: reduce_slabs(): lax.ppermute(sent, 'col', [(c, (c + 2 * shift) % col_count) for c in rang...]
    reduce_scatter x1 -> x0, waiting for transfers between devices: 151 us -> none  [local(): lax.psum_scatter(own_probe, 'col', scatter_dimension=1, tiled=True)]
    all_gather x2 -> x1, waiting for transfers between devices: 92.8 us -> 0.01 us  [local(): all_kids = lax.all_gather(kid_share, 'row', axis=1, tiled=True)]
    all_to_all x0 -> x3, waiting for transfers between devices: none -> 54.8 us  [the longest x1 21.5 us: local(): lax.all_to_all(core.reshape(col_count, probes // col_count, probes), 'col...]
    all_to_all x0 -> x3, starting transfers between devices: none -> 45.9 us  [the longest x1 29.7 us: local(): lax.all_to_all(core.reshape(col_count, probes // col_count, probes), 'col...]
  transfers between devices with their start and end apart: 6 -> 17, of which waited for: 6 -> 9; matrix products, arithmetic and copies ran while one was open for 3% -> 16% of each run, Pallas kernels for 0% -> 8%
where the time goes in v1:
time: 514 us; the launch traced here: 505 us
  waiting for transfers between devices  225 us (44%)
  starting transfers between devices  79.9 us (16%)
  matrix products  73.5 us (14%)
  local copies, waits for them, and re-layouts  50.8 us (10%)
  Pallas kernels  42.2 us (8%)
  other arithmetic  18.6 us (4%)
  between operations  14.5 us (3%)
    ppermute x6, waiting for transfers between devices, reduce_slabs(): lax.ppermute(sent, 'col', [(c, (c + 2 * shift) % col_count) for c in rang...  150 us
    pallas_call x1, Pallas kernels, leaf_basis_of(): pl.pallas_call(functools.partial(basis_kernel, math.sqrt(LEAF)), out_shap...  42.2 us
    dot_general x1, matrix products, local(): jnp.dot(parent_front, parent_test, preferred_element_type=jnp.float32)  34.9 us
    all_to_all x1, starting transfers between devices, local(): lax.all_to_all(core.reshape(col_count, probes // col_count, probes), 'col...  29.7 us
    ppermute x4, starting transfers between devices, local(): pieces.append(lax.ppermute(tile, ('row', 'col'), routes))  23.7 us
    all_to_all x1, waiting for transfers between devices, local(): lax.all_to_all(core.reshape(col_count, probes // col_count, probes), 'col...  21.5 us
    dot_general x1, matrix products, local(): jnp.einsum('cmk,ckr->cmr', child_update, child_test, preferred_element_ty...  21.4 us
    ppermute x2, waiting for transfers between devices, reduce_slabs(): lax.ppermute(lax.dynamic_index_in_dim(view, 1 - parity, 2, False), 'col',...  20.5 us
  transfers between devices with their start and end apart: 17, of which 9 were waited for; matrix products, arithmetic and copies ran while one was open for 16% of the time, Pallas kernels for 8%

profile of v1, /device:TPU:0, one launch (start us, length us, event | category | flops | bytes accessed | tf_op | source)
XLA Modules:
  0.0 504.7 jit_solution(7592665603311462473)
XLA Ops:
  7.2 0.0 copy-start
  7.2 0.0 all-gather.2.cloned.1.call-start
  7.2 1.8 copy-done
  9.1 21.4 %fusion.33 = f32[2,3584,448]{2,1,0:T(8,128)} fusion(bf16[2,3584,1792]{2,1,0:T(8,128)(2,1)} %param.6, bf16[2,1792,448]{1,2,0:T(8,128)(2,1)S(1)} %copy-done), kind=kOutput, calls=%fused_computation.53 | convolution fusion | flops 11509170176 | bytes 41746432 | tf_op jit(solution)/shard_map/cmk,ckr->cmr/dot_general | solution.py:141
  30.5 7.7 %dynamic-slice_bitcast_fusion = f32[56,4,16,448]{3,2,1,0:T(8,128)} fusion(f32[56,4,2,16,448]{4,3,2,1,0:T(8,128)} %bitcast.92, s32[]{:T(128)S(6)} %select_n.134), kind=kLoop, calls=%fused_computation.2 | loop fusion | bytes 12845060 | tf_op jit(solution)/shard_map/jit(dynamic_index_in_dim)/squeeze | solution.py:106
  38.2 0.5 collective-permute-start.4
  38.7 11.6 %collective-permute-done.4 = f32[56,4,16,448]{3,2,1,0:T(8,128)} collective-permute-done((f32[56,4,16,448]{3,2,1,0:T(8,128)}, f32[56,4,16,448]{3,2,1,0:T(8,128)}, u32[]{:S(2)}, u32[]{:S(2)}) %collective-permute-start.4) | collective-permute-done | bytes 6422560 | tf_op jit(solution)/shard_map/ppermute | solution.py:105
  50.3 6.5 %fusion.4 = (bf16[56,16,448]{2,1,0:T(8,128)(2,1)S(1)}, bf16[56,16,448]{2,1,0:T(8,128)(2,1)}, bf16[56,16,448]{2,1,0:T(8,128)(2,1)}) fusion(f32[56,4,16,448]{3,2,1,0:T(8,128)} %collective-permute-done.4, s32[]{:T(128)S(6)} %select_n.136, f32[56,4,2,16,448]{4,3,2,1,0:T(8,128)} %bitcast.93, s32[]{:T(128)S(6)} %select_n.137, s32[]{:T(128)S(6)} %select_n.133, ...), kind=kLoop, calls=%fused_computation.10 | loop fusion | flops 2408448 | bytes 12042268 | tf_op jit(solution)/shard_map/convert_element_type | solution.py:119
  56.8 5.0 collective-permute-start.7
  61.8 0.0 collective-permute-start.6
  61.8 1.2 collective-permute-start.5
  62.9 20.0 %collective-permute-done.7 = bf16[56,16,448]{2,1,0:T(8,128)(2,1)S(1)} collective-permute-done((bf16[56,16,448]{2,1,0:T(8,128)(2,1)}, bf16[56,16,448]{2,1,0:T(8,128)(2,1)S(1)}, u32[]{:S(2)}, u32[]{:S(2)}) %collective-permute-start.7) | collective-permute-done | bytes 802848 | tf_op jit(solution)/shard_map/ppermute | solution.py:120
  82.9 57.9 %collective-permute-done.6 = bf16[56,16,448]{2,1,0:T(8,128)(2,1)S(1)} collective-permute-done((bf16[56,16,448]{2,1,0:T(8,128)(2,1)}, bf16[56,16,448]{2,1,0:T(8,128)(2,1)S(1)}, u32[]{:S(2)}, u32[]{:S(2)}) %collective-permute-start.6) | collective-permute-done | bytes 802848 | tf_op jit(solution)/shard_map/ppermute | solution.py:120
  140.8 0.9 copy-done.4
  141.7 0.0 collective-permute-done.5
  141.7 3.5 fusion.7
  145.2 1.5 copy.56
  146.6 0.0 all-gather.2.cloned.1.call-update
  146.7 34.9 %fusion.32 = f32[7168,448]{1,0:T(8,128)} fusion(bf16[7168,3584]{1,0:T(8,128)(2,1)} %param.5, bf16[3584,448]{0,1:T(8,128)(2,1)} %param.7), kind=kOutput, calls=%fused_computation.52 | convolution fusion | flops 23018340352 | bytes 67436544 | tf_op jit(solution)/shard_map/dot_general | solution.py:149
  181.6 9.7 %dynamic-slice_bitcast_fusion.1 = f32[56,4,16,448]{3,2,1,0:T(8,128)} fusion(f32[56,4,2,16,448]{4,3,2,1,0:T(8,128)} %bitcast.95, s32[]{:T(128)S(6)} %select_n.134), kind=kLoop, calls=%fused_computation.3 | loop fusion | bytes 12845060 | tf_op jit(solution)/shard_map/jit(dynamic_index_in_dim)/squeeze | solution.py:106
  191.2 0.0 collective-permute-start
  191.3 1.5 copy-done.2
  192.7 1.6 constant_dynamic-slice_fusion.6
  194.4 8.9 %collective-permute-done = f32[56,4,16,448]{3,2,1,0:T(8,128)} collective-permute-done((f32[56,4,16,448]{3,2,1,0:T(8,128)}, f32[56,4,16,448]{3,2,1,0:T(8,128)}, u32[]{:S(2)}, u32[]{:S(2)}) %collective-permute-start) | collective-permute-done | bytes 6422560 | tf_op jit(solution)/shard_map/ppermute | solution.py:105
  203.3 6.0 %constant_dynamic-slice_fusion.5 = (f32[56,1,16,448]{3,2,1,0:T(8,128)S(1)}, f32[56,1,16,448]{3,2,1,0:T(8,128)S(1)}, f32[56,1,16,448]{3,2,1,0:T(8,128)S(1)}, f32[56,1,16,448]{3,2,1,0:T(8,128)}) fusion(f32[56,4,16,448]{3,2,1,0:T(8,128)} %collective-permute-done, s32[]{:T(128)S(6)} %select_n.136, s32[]{:T(128)S(6)} %select_n.142, s32[]{:T(128)S(6)} %select_n.139, ...), kind=kLoop, calls=%fused_computation.43 | loop fusion | bytes 12845072 | tf_op jit(solution)/shard_map/jit(dynamic_index_in_dim)/dynamic_slice | solution.py:113
  209.3 2.9 fusion.8
  212.2 0.4 collective-permute-start.3
  212.6 2.9 fusion.9
  215.4 1.2 collective-permute-start.2
  216.6 2.9 fusion.10
  219.5 2.0 collective-permute-start.1
  221.5 14.5 %collective-permute-done.3 = bf16[56,16,448]{2,0,1:T(8,128)(2,1)S(1)} collective-permute-done((bf16[56,16,448]{2,0,1:T(8,128)(2,1)}, bf16[56,16,448]{2,0,1:T(8,128)(2,1)S(1)}, u32[]{:S(2)}, u32[]{:S(2)}) %collective-permute-start.3) | collective-permute-done | bytes 802848 | tf_op jit(solution)/shard_map/ppermute | solution.py:120
  236.1 57.6 %collective-permute-done.2 = bf16[56,16,448]{2,0,1:T(8,128)(2,1)} collective-permute-done((bf16[56,16,448]{2,0,1:T(8,128)(2,1)}, bf16[56,16,448]{2,0,1:T(8,128)(2,1)}, u32[]{:S(2)}, u32[]{:S(2)}) %collective-permute-start.2) | collective-permute-done | bytes 802848 | tf_op jit(solution)/shard_map/ppermute | solution.py:120
  293.7 0.0 collective-permute-done.1
  293.7 12.9 %bitcast_add_fusion = f32[56,16,448]{2,0,1:T(8,128)S(1)} fusion(f32[56,1,16,448]{3,2,1,0:T(8,128)} %get-tuple-element.16, f32[56,1,1,16,448]{4,3,2,1,0:T(8,128)S(1)} %get-tuple-element.12, bf16[56,16,448]{2,0,1:T(8,128)(2,1)S(1)} %collective-permute-done.3, bf16[56,16,448]{2,0,1:T(8,128)(2,1)} %collective-permute-done.2, ...), kind=kOutput, calls=%fused_computation.4 | convolution fusion | flops 1082208512 | bytes 13648768 | tf_op jit(solution)/shard_map/cpn,cnsr->psr/dot_general | solution.py:155
  306.6 2.3 copy.58
  308.9 3.6 all-to-all-start
  312.6 5.7 %constant_dynamic-slice_fusion = (bf16[896,896]{1,0:T(8,128)(2,1)}, bf16[896,896]{1,0:T(8,128)(2,1)}, bf16[896,896]{1,0:T(8,128)(2,1)}, bf16[896,896]{1,0:T(8,128)(2,1)}) fusion(bf16[7168,3584]{1,0:T(8,128)(2,1)} %param.5, s32[]{:T(128)S(6)} %select_n.155, s32[]{:T(128)S(6)} %select_n.150, s32[]{:T(128)S(6)} %select_n.147, s32[]{:T(128)S(6)} %select_n.153), kind=kLoop, calls=%fused_computation.38 | loop fusion | bytes 12845072 | tf_op jit(solution)/shard_map/dynamic_slice | solution.py:166
  318.4 4.9 collective-permute-start.8
  323.3 2.5 collective-permute-start.9
  325.7 13.7 %collective-permute-start.10 = (bf16[896,896]{1,0:T(8,128)(2,1)}, bf16[896,896]{1,0:T(8,128)(2,1)}, u32[]{:S(2)}, u32[]{:S(2)}) collective-permute-start(bf16[896,896]{1,0:T(8,128)(2,1)} %get-tuple-element.5), channel_id=1, source_target_pairs={{0,0},{1,4},{10,8},{11,12},{20,16},{21,20},{30,24},{31,28}} | collective-permute-start | bytes 4816904 | tf_op jit(solution)/shard_map/ppermute | solution.py:175
  339.4 2.7 collective-permute-start.11
  342.1 13.8 %all-to-all-done = f32[8,112,448]{2,1,0:T(8,128)S(1)} async-done(((f32[8,112,448]{2,1,0:T(8,128)}), f32[8,112,448]{2,1,0:T(8,128)S(1)}, u32[]{:S(2)}, u32[]{:S(2)}) %all-to-all-start) | async-done | bytes 1605664 | tf_op jit(solution)/shard_map/all_to_all | solution.py:159
  355.9 1.3 copy-done.3
  357.1 2.0 copy.68
  359.1 42.2 %leaf_basis.1 = bf16[448,896]{1,0:T(8,128)(2,1)S(1)} custom-call(f32[448,896]{1,0:T(8,128)S(1)} %bitcast.91), custom_call_target="tpu_custom_call" | custom-call | flops 7193231360 | bytes 2408448 | tf_op jit(solution)/shard_map/leaf_basis/pallas_call | solution.py:78
  401.3 0.8 copy.62
  402.0 0.1 copy.63
  402.1 1.2 copy.64
  403.3 0.0 collective-permute-start.12
  403.4 1.0 reshape.52
  404.4 1.1 copy.60
  405.5 12.6 %all-to-all-start.1 = ((bf16[8,112,448]{1,2,0:T(8,128)(2,1)}), bf16[8,112,448]{1,2,0:T(8,128)(2,1)}, u32[]{:S(2)}, u32[]{:S(2)}) async-start(bf16[8,112,448]{1,2,0:T(8,128)(2,1)} %copy.60), calls=%async_computation.1 | async-start | bytes 1835008 | tf_op jit(solution)/shard_map/all_to_all | solution.py:183
  418.1 0.0 collective-permute-done.8
  418.1 0.0 collective-permute-done.9
  418.1 0.0 collective-permute-done.10
  418.1 0.0 collective-permute-done.11
  418.2 0.0 collective-permute-done.12
  418.2 4.2 convolution_multiply_fusion
  422.4 19.6 %all-to-all-done.1 = bf16[8,112,448]{1,2,0:T(8,128)(2,1)} async-done(((bf16[8,112,448]{1,2,0:T(8,128)(2,1)}), bf16[8,112,448]{1,2,0:T(8,128)(2,1)}, u32[]{:S(2)}, u32[]{:S(2)}) %all-to-all-start.1) | async-done | bytes 802848 | tf_op jit(solution)/shard_map/all_to_all | solution.py:183
  442.0 29.7 %all-to-all-start.2 = ((f32[8,56,448]{2,1,0:T(8,128)}), f32[8,56,448]{2,1,0:T(8,128)}, u32[]{:S(2)}, u32[]{:S(2)}) async-start(f32[8,56,448]{2,1,0:T(8,128)} %bitcast.102), calls=%async_computation.2 | async-start | bytes 1835008 | tf_op jit(solution)/shard_map/all_to_all | solution.py:204
  471.7 2.4 copy.61
  474.0 21.5 %all-to-all-done.2 = f32[8,56,448]{2,1,0:T(8,128)} async-done(((f32[8,56,448]{2,1,0:T(8,128)}), f32[8,56,448]{2,1,0:T(8,128)}, u32[]{:S(2)}, u32[]{:S(2)}) %all-to-all-start.2) | async-done | bytes 802848 | tf_op jit(solution)/shard_map/all_to_all | solution.py:204
  495.5 2.2 copy.82
  (9 shorter events, 0.0 us)
Async XLA Ops:
  7.2 1.9 copy-start
  7.2 286.5 %all-gather.2.cloned.1.call-start = ((), (), s32[]{:S(2)}) async-start(), calls=%async_computation.3 | async-start | bytes 9175040 | tf_op jit(solution)/shard_map/all_gather | solution.py:147
  38.2 12.1 %collective-permute-start.4 = (f32[56,4,16,448]{3,2,1,0:T(8,128)}, f32[56,4,16,448]{3,2,1,0:T(8,128)}, u32[]{:S(2)}, u32[]{:S(2)}) collective-permute-start(f32[56,4,16,448]{3,2,1,0:T(8,128)} %dynamic-slice_bitcast_fusion), channel_id=1, source_target_pairs={{0,1},{1,0},{2,3},{3,2},{4,5},{5,4},{6,7},{7,6},{8,9},{9,8},{10,11... | collective-permute-start | bytes 19267592 | tf_op jit(solution)/shard_map/ppermute | solution.py:105
  56.8 26.1 %collective-permute-start.7 = (bf16[56,16,448]{2,1,0:T(8,128)(2,1)}, bf16[56,16,448]{2,1,0:T(8,128)(2,1)S(1)}, u32[]{:S(2)}, u32[]{:S(2)}) collective-permute-start(bf16[56,16,448]{2,1,0:T(8,128)(2,1)} %get-tuple-element.7), channel_id=1, source_target_pairs={{0,6},{1,7},{2,0},{3,1},{4,2},{5,3},{6,4},{7,5},{8,14},{9,15},{10,... | collective-permute-start | bytes 2408456 | tf_op jit(solution)/shard_map/ppermute | solution.py:120
  61.8 79.0 %collective-permute-start.6 = (bf16[56,16,448]{2,1,0:T(8,128)(2,1)}, bf16[56,16,448]{2,1,0:T(8,128)(2,1)S(1)}, u32[]{:S(2)}, u32[]{:S(2)}) collective-permute-start(bf16[56,16,448]{2,1,0:T(8,128)(2,1)} %get-tuple-element.8), channel_id=1, source_target_pairs={{0,4},{1,5},{2,6},{3,7},{4,0},{5,1},{6,2},{7,3},{8,12},{9,13},{10,... | collective-permute-start | bytes 2408456 | tf_op jit(solution)/shard_map/ppermute | solution.py:120
  61.8 79.9 %collective-permute-start.5 = (bf16[56,16,448]{2,1,0:T(8,128)(2,1)S(1)}, bf16[56,16,448]{2,1,0:T(8,128)(2,1)}, u32[]{:S(2)}, u32[]{:S(2)}) collective-permute-start(bf16[56,16,448]{2,1,0:T(8,128)(2,1)S(1)} %get-tuple-element.6), channel_id=1, source_target_pairs={{0,2},{1,3},{2,4},{3,5},{4,6},{5,7},{6,0},{7,1},{8,10},{9,11},{10,... | collective-permute-start | bytes 2408456 | tf_op jit(solution)/shard_map/ppermute | solution.py:120
  140.8 0.9 copy-start.4
  181.6 11.2 %copy-start.2 = (f32[7168,448]{1,0:T(8,128)S(1)}, f32[7168,448]{1,0:T(8,128)}, u32[]{:S(2)}) copy-start(f32[7168,448]{1,0:T(8,128)} %fusion.32) | copy-start | bytes 38535172
  191.2 12.0 %collective-permute-start = (f32[56,4,16,448]{3,2,1,0:T(8,128)}, f32[56,4,16,448]{3,2,1,0:T(8,128)}, u32[]{:S(2)}, u32[]{:S(2)}) collective-permute-start(f32[56,4,16,448]{3,2,1,0:T(8,128)} %dynamic-slice_bitcast_fusion.1), channel_id=1, source_target_pairs={{0,1},{1,0},{2,3},{3,2},{4,5},{5,4},{6,7},{7,6},{8,9},{9,8},{10,11... | collective-permute-start | bytes 19267592 | tf_op jit(solution)/shard_map/ppermute | solution.py:105
  212.2 23.9 %collective-permute-start.3 = (bf16[56,16,448]{2,0,1:T(8,128)(2,1)}, bf16[56,16,448]{2,0,1:T(8,128)(2,1)S(1)}, u32[]{:S(2)}, u32[]{:S(2)}) collective-permute-start(bf16[56,16,448]{2,0,1:T(8,128)(2,1)} %fusion.8), channel_id=1, source_target_pairs={{0,6},{1,7},{2,0},{3,1},{4,2},{5,3},{6,4},{7,5},{8,14},{9,15},{10,... | collective-permute-start | bytes 2408456 | tf_op jit(solution)/shard_map/ppermute | solution.py:120
  215.4 78.3 %collective-permute-start.2 = (bf16[56,16,448]{2,0,1:T(8,128)(2,1)}, bf16[56,16,448]{2,0,1:T(8,128)(2,1)}, u32[]{:S(2)}, u32[]{:S(2)}) collective-permute-start(bf16[56,16,448]{2,0,1:T(8,128)(2,1)} %fusion.9), channel_id=1, source_target_pairs={{0,4},{1,5},{2,6},{3,7},{4,0},{5,1},{6,2},{7,3},{8,12},{9,13},{10,... | collective-permute-start | bytes 2408456 | tf_op jit(solution)/shard_map/ppermute | solution.py:120
  216.6 4.9 copy-start.5
  219.5 74.2 %collective-permute-start.1 = (bf16[56,16,448]{2,0,1:T(8,128)(2,1)}, bf16[56,16,448]{2,0,1:T(8,128)(2,1)}, u32[]{:S(2)}, u32[]{:S(2)}) collective-permute-start(bf16[56,16,448]{2,0,1:T(8,128)(2,1)} %fusion.10), channel_id=1, source_target_pairs={{0,2},{1,3},{2,4},{3,5},{4,6},{5,7},{6,0},{7,1},{8,10},{9,11},{10,... | collective-permute-start | bytes 2408456 | tf_op jit(solution)/shard_map/ppermute | solution.py:120
  308.9 46.9 %all-to-all-start = ((f32[8,112,448]{2,1,0:T(8,128)}), f32[8,112,448]{2,1,0:T(8,128)S(1)}, u32[]{:S(2)}, u32[]{:S(2)}) async-start(f32[8,112,448]{2,1,0:T(8,128)} %bitcast.24), calls=%async_computation | async-start | bytes 3670016 | tf_op jit(solution)/shard_map/all_to_all | solution.py:159
  318.4 99.8 %collective-permute-start.8 = (bf16[896,896]{1,0:T(8,128)(2,1)}, bf16[896,896]{1,0:T(8,128)(2,1)}, u32[]{:S(2)}, u32[]{:S(2)}) collective-permute-start(bf16[896,896]{1,0:T(8,128)(2,1)} %get-tuple-element.4), channel_id=1, source_target_pairs={{0,2},{1,6},{10,10},{11,14},{20,18},{21,22},{30,26},{31,30}} | collective-permute-start | bytes 4816904 | tf_op jit(solution)/shard_map/ppermute | solution.py:175
  323.3 94.9 %collective-permute-start.9 = (bf16[896,896]{1,0:T(8,128)(2,1)}, bf16[896,896]{1,0:T(8,128)(2,1)}, u32[]{:S(2)}, u32[]{:S(2)}) collective-permute-start(bf16[896,896]{1,0:T(8,128)(2,1)} %get-tuple-element.3), channel_id=1, source_target_pairs={{0,3},{1,7},{10,11},{11,15},{20,19},{21,23},{30,27},{31,31}} | collective-permute-start | bytes 4816904 | tf_op jit(solution)/shard_map/ppermute | solution.py:175
  325.7 92.4 %collective-permute-start.10 = (bf16[896,896]{1,0:T(8,128)(2,1)}, bf16[896,896]{1,0:T(8,128)(2,1)}, u32[]{:S(2)}, u32[]{:S(2)}) collective-permute-start(bf16[896,896]{1,0:T(8,128)(2,1)} %get-tuple-element.5), channel_id=1, source_target_pairs={{0,0},{1,4},{10,8},{11,12},{20,16},{21,20},{30,24},{31,28}} | collective-permute-start | bytes 4816904 | tf_op jit(solution)/shard_map/ppermute | solution.py:175
  339.4 78.7 %collective-permute-start.11 = (bf16[896,896]{1,0:T(8,128)(2,1)}, bf16[896,896]{1,0:T(8,128)(2,1)}, u32[]{:S(2)}, u32[]{:S(2)}) collective-permute-start(bf16[896,896]{1,0:T(8,128)(2,1)} %get-tuple-element.2), channel_id=1, source_target_pairs={{0,1},{1,5},{10,9},{11,13},{20,17},{21,21},{30,25},{31,29}} | collective-permute-start | bytes 4816904 | tf_op jit(solution)/shard_map/ppermute | solution.py:175
  355.9 1.3 copy-start.3
  403.3 14.8 %collective-permute-start.12 = (bf16[896,448]{0,1:T(8,128)(2,1)}, bf16[896,448]{0,1:T(8,128)(2,1)}, u32[]{:S(2)}, u32[]{:S(2)}) collective-permute-start(bf16[896,448]{0,1:T(8,128)(2,1)} %copy.64), channel_id=1, source_target_pairs={{0,1},{1,0},{2,3},{3,2},{4,5},{5,4},{6,7},{7,6},{8,9},{9,8},{10,11... | collective-permute-start | bytes 2408456 | tf_op jit(solution)/shard_map/ppermute | solution.py:193
  405.5 36.5 %all-to-all-start.1 = ((bf16[8,112,448]{1,2,0:T(8,128)(2,1)}), bf16[8,112,448]{1,2,0:T(8,128)(2,1)}, u32[]{:S(2)}, u32[]{:S(2)}) async-start(bf16[8,112,448]{1,2,0:T(8,128)(2,1)} %copy.60), calls=%async_computation.1 | async-start | bytes 1835008 | tf_op jit(solution)/shard_map/all_to_all | solution.py:183
  442.0 53.5 %all-to-all-start.2 = ((f32[8,56,448]{2,1,0:T(8,128)}), f32[8,56,448]{2,1,0:T(8,128)}, u32[]{:S(2)}, u32[]{:S(2)}) async-start(f32[8,56,448]{2,1,0:T(8,128)} %bitcast.102), calls=%async_computation.2 | async-start | bytes 1835008 | tf_op jit(solution)/shard_map/all_to_all | solution.py:204
  471.7 26.0 %copy-start.1 = (bf16[2,1792,448]{1,2,0:T(8,128)(2,1)S(1)}, bf16[2,1792,448]{1,2,0:T(8,128)(2,1)}, u32[]{:S(2)}) copy-start(bf16[2,1792,448]{1,2,0:T(8,128)(2,1)} %param.8) | copy-start | bytes 9633796
Sparse Core Ops, SparseCore 0:
  146.8 78.3 all-gather.1

commit v2 on v1

--- a/solution.py
+++ b/solution.py
@@ -7,6 +7,7 @@
 from jax.experimental import pallas as pl
 from jax.experimental.pallas import tpu as pltpu
 from jax.sharding import PartitionSpec as P
+
 
 LEAF = 896
 BLOCK = 128
@@ -94,34 +95,72 @@
     )(yt)
 
 
-def reduce_slabs(partial, col_count, col_index):
-    blocks = partial.shape[0] // BLOCK
-    slab = BLOCK // col_count
+def probe_kernel(parity_ref, front_ref, test_ref, kept_ref, sent_ref):
+    total = jnp.dot(front_ref[...], test_ref[...], preferred_element_type=jnp.float32)
+    blocks, pairs, slab, probes = kept_ref.shape
+    view = total.reshape(blocks * pairs, 2, slab, probes)
+    even = parity_ref[0] == 0
+    kept_ref[...] = jnp.where(even, view[:, 0], view[:, 1]).reshape(kept_ref.shape)
+    sent_ref[...] = jnp.where(even, view[:, 1], view[:, 0]).reshape(sent_ref.shape)
+
+
+def probe(front, test, which, first_row, rows, col_count, parity):
+    depth, probes = test.shape[1:]
+    tile = max(t for t in range(BLOCK, 4 * BLOCK + 1, BLOCK) if rows % t == 0)
+    pairs, slab = col_count // 2, BLOCK // col_count
+    half = jax.ShapeDtypeStruct((rows // BLOCK, pairs, slab, probes), jnp.float32)
+    out_spec = pl.BlockSpec((tile // BLOCK, pairs, slab, probes), lambda i, p: (i, 0, 0, 0))
+    skip = first_row // tile
+    return pl.pallas_call(
+        probe_kernel,
+        out_shape=(half, half),
+        grid_spec=pltpu.PrefetchScalarGridSpec(
+            num_scalar_prefetch=1,
+            grid=(rows // tile,),
+            in_specs=[
+                pl.BlockSpec((None, tile, depth), lambda i, p: (which, skip + i, 0)),
+                pl.BlockSpec((None, depth, probes), lambda i, p: (which, 0, 0)),
+            ],
+            out_specs=(out_spec, out_spec),
+        ),
+        compiler_params=pltpu.CompilerParams(vmem_limit_bytes=40 << 20),
+        cost_estimate=pl.CostEstimate(
+            flops=2 * rows * depth * probes,
+            bytes_accessed=2 * rows * depth + 2 * depth * probes + 4 * rows * probes,
+            transcendentals=0,
+        ),
+        name="probe",
+    )(parity, front, test)
+
+
+def swap_pair(halves, col_count):
+    kept, sent = halves
+    return kept, lax.ppermute(sent, "col", [(c, c ^ 1) for c in range(col_count)])
+
+
+def send_pairs(kept, swapped, col_count, pair_index):
     pairs = col_count // 2
-    probes = partial.shape[1]
-    pair_index = col_index // 2
-    parity = col_index % 2
-    view = partial.reshape(blocks, pairs, 2, slab, probes)
-    swapped = lax.ppermute(
-        lax.dynamic_index_in_dim(view, 1 - parity, 2, False),
-        "col",
-        [(c, c ^ 1) for c in range(col_count)],
-    )
-    kept = lax.dynamic_index_in_dim(view, parity, 2, False)
 
     def piece(pair):
         return lax.dynamic_index_in_dim(kept, pair, 1, False) + lax.dynamic_index_in_dim(
             swapped, pair, 1, False
         )
 
-    total = piece(pair_index)
-    for shift in range(1, pairs):
-        sent = piece((pair_index + shift) % pairs).astype(jnp.bfloat16)
-        came = lax.ppermute(
-            sent, "col", [(c, (c + 2 * shift) % col_count) for c in range(col_count)]
-        )
-        total = total + came.astype(jnp.float32)
-    return total
+    came = [
+        lax.ppermute(
+            piece((pair_index + shift) % pairs).astype(jnp.bfloat16),
+            "col",
+            [(c, (c + 2 * shift) % col_count) for c in range(col_count)],
+        )
+        for shift in range(1, pairs)
+    ]
+    return piece(pair_index), came
+
+
+def add_up(own, came):
+    for term in came:
+        own = own + term.astype(jnp.float32)
+    return own
 
 
 def local(parent_front, child_update, parent_test, child_test, child_map):
@@ -131,36 +170,21 @@
     col_index = lax.axis_index("col")
     slab = BLOCK // col_count
     own_blocks = parent_front.shape[0] // BLOCK
-    kid_blocks = child_update.shape[1] // BLOCK
     probes = parent_test.shape[1]
     per_leaf = LEAF // BLOCK
     leaf_count = own_blocks // per_leaf
     col_leaves = parent_front.shape[1] // LEAF
     shrink = 1.0 / math.sqrt(LEAF)
 
-    kid_probe = jnp.einsum(
-        "cmk,ckr->cmr", child_update, child_test, preferred_element_type=jnp.float32
-    )
-    kid_share = reduce_slabs(
-        kid_probe.reshape(2 * kid_blocks * BLOCK, probes), col_count, col_index
-    ).reshape(2, kid_blocks, slab, probes)
-    all_kids = lax.all_gather(kid_share, "row", axis=1, tiled=True)
-
-    own_probe = jnp.dot(parent_front, parent_test, preferred_element_type=jnp.float32)
-    own_share = reduce_slabs(own_probe, col_count, col_index)
-
-    targets = jnp.arange(own_blocks, dtype=jnp.int32)
-    mapped = child_map - row_index * own_blocks
-    onehot = (mapped[:, None, :] == targets[None, :, None]).astype(jnp.float32)
-    sample = own_share + jnp.einsum("cpn,cnsr->psr", onehot, all_kids, precision=HIGH)
-
-    by_leaf = sample.reshape(leaf_count, per_leaf * slab, probes)
-    by_leaf = jnp.pad(by_leaf, ((0, col_count - leaf_count), (0, 0), (0, 0)))
-    leaf_rows = lax.all_to_all(by_leaf, "col", 0, 0, tiled=True).reshape(LEAF, probes)
-
-    front = parent_front
-    pieces = []
-    for position in range(col_leaves):
+    tie = lax.optimization_barrier
+    pair_index = col_index // 2
+    parity = col_index % 2
+    half = own_blocks // 2 * BLOCK
+    sign = jnp.reshape(parity, (1,)).astype(jnp.int32)
+    fronts, tests = parent_front[None], parent_test[None]
+    kid_rows = child_update.shape[1]
+
+    def send_tile(position, front):
         sibling = col_index * col_leaves + position
         row_start = jnp.bitwise_xor(sibling, 1) % leaf_count * LEAF
         tile = lax.dynamic_slice(front, (row_start, position * LEAF), (LEAF, LEAF))
@@ -172,7 +196,40 @@
                     routes.append(
                         (row * col_count + other // col_leaves, row * col_count + slot)
                     )
-        pieces.append(lax.ppermute(tile, ("row", "col"), routes))
+        return lax.ppermute(tile, ("row", "col"), routes)
+
+    pieces = {position: send_tile(position, parent_front) for position in range(0, col_leaves, 2)}
+
+    jobs = (
+        (child_update, child_test, 0, 0, kid_rows),
+        (child_update, child_test, 1, 0, kid_rows),
+        (fronts, tests, 0, 0, half),
+        (fronts, tests, 0, half, half),
+    )
+    sums = []
+    for front, test, which, first_row, rows in jobs:
+        halves = probe(front, test, which, first_row, rows, col_count, sign)
+        kept, swapped = swap_pair(halves, col_count)
+        sums.append(send_pairs(kept, swapped, col_count, pair_index))
+    (first_own, first_came), (second_own, second_came) = sums[:2]
+    (upper_own, upper_came), (lower_own, lower_came) = sums[2:]
+
+    kid_share = jnp.stack([add_up(first_own, first_came), add_up(second_own, second_came)])
+    all_kids = lax.all_gather(kid_share, "row", axis=1, tiled=True)
+    own_share = jnp.concatenate([add_up(upper_own, upper_came), add_up(lower_own, lower_came)])
+
+    targets = jnp.arange(own_blocks, dtype=jnp.int32)
+    mapped = child_map - row_index * own_blocks
+    onehot = (mapped[:, None, :] == targets[None, :, None]).astype(jnp.float32)
+    sample = own_share + jnp.einsum("cpn,cnsr->psr", onehot, all_kids, precision=HIGH)
+
+    by_leaf = sample.reshape(leaf_count, per_leaf * slab, probes)
+    by_leaf = jnp.pad(by_leaf, ((0, col_count - leaf_count), (0, 0), (0, 0)))
+    leaf_rows = lax.all_to_all(by_leaf, "col", 0, 0, tiled=True).reshape(LEAF, probes)
+
+    leaf_rows, front = tie((leaf_rows, parent_front))
+    for position in range(1, col_leaves, 2):
+        pieces[position] = send_tile(position, front)
     wanted = jnp.bitwise_xor(col_index, 1) % col_leaves
     front_tile = pieces[0]
     for position in range(1, col_leaves):

time: 514 us -> 479 us (0.932); the launches traced: 505 us -> 476 us
  matrix products: 73.5 us -> 14.1 us
  Pallas kernels: 42.2 us -> 99.6 us
  waiting for transfers between devices: 225 us -> 175 us
  starting transfers between devices: 79.9 us -> 102 us
  other arithmetic: 18.6 us -> 26.1 us
  local copies, waits for them, and re-layouts: 50.8 us -> 44.2 us
    ppermute x12 -> x20, waiting for transfers between devices: 171 us -> 104 us  [the longest x12 104 us: send_pairs(): lax.ppermute(piece((pair_index + shift) % pairs).astype(jnp.bfloat16), 'c...]
    pallas_call x0 -> x4, Pallas kernels: none -> 57.5 us  [probe(): pl.pallas_call(probe_kernel, out_shape=(half, half), grid_spec=pltpu.Pref...]
    dot_general x2 -> x0, matrix products: 56.3 us -> none  [the longest x1 34.9 us: local(): jnp.dot(parent_front, parent_test, preferred_element_type=jnp.float32)]
    ppermute x12 -> x20, starting transfers between devices: 33.9 us -> 78 us  [the longest x12 41.9 us: send_pairs(): lax.ppermute(piece((pair_index + shift) % pairs).astype(jnp.bfloat16), 'c...]
    all_to_all x1, starting transfers between devices: 29.7 us -> 8.88 us  [local(): lax.all_to_all(core.reshape(col_count, probes // col_count, probes), 'col...]
    squeeze x2 -> x0, local copies, waits for them, and re-layouts: 17.4 us -> none  [reduce_slabs(): lax.dynamic_index_in_dim(view, 1 - parity, 2, False)]
    all_to_all x1, waiting for transfers between devices: 13.8 us -> 29.7 us  [local(): lax.all_to_all(by_leaf, 'col', 0, 0, tiled=True).reshape(LEAF, probes)]
    unnamed x13 -> x25, local copies, waits for them, and re-layouts: 7.66 us -> 19.3 us
  transfers between devices with their start and end apart: 17 -> 25, of which waited for: 9 -> 10; matrix products, arithmetic and copies ran while one was open for 16% -> 10% of each run, Pallas kernels for 8% -> 19%
where the time goes in v2:
time: 479 us; the launch traced here: 476 us
  waiting for transfers between devices  175 us (37%)
  starting transfers between devices  102 us (21%)
  Pallas kernels  99.6 us (21%)
  local copies, waits for them, and re-layouts  44.2 us (9%)
  other arithmetic  26.1 us (5%)
  between operations  14.3 us (3%)
  matrix products  14.1 us (3%)
    ppermute x12, waiting for transfers between devices, send_pairs(): lax.ppermute(piece((pair_index + shift) % pairs).astype(jnp.bfloat16), 'c...  104 us
    pallas_call x4, Pallas kernels, probe(): pl.pallas_call(probe_kernel, out_shape=(half, half), grid_spec=pltpu.Pref...  57.5 us
    pallas_call x1, Pallas kernels, leaf_basis_of(): pl.pallas_call(functools.partial(basis_kernel, math.sqrt(LEAF)), out_shap...  42.2 us
    ppermute x12, starting transfers between devices, send_pairs(): lax.ppermute(piece((pair_index + shift) % pairs).astype(jnp.bfloat16), 'c...  41.9 us
    ppermute x4, starting transfers between devices, send_tile(): return lax.ppermute(tile, ('row', 'col'), routes)  35.1 us
    all_to_all x1, waiting for transfers between devices, local(): lax.all_to_all(by_leaf, 'col', 0, 0, tiled=True).reshape(LEAF, probes)  29.7 us
    all_to_all x1, waiting for transfers between devices, local(): lax.all_to_all(core.reshape(col_count, probes // col_count, probes), 'col...  22.5 us
    all_to_all x1, waiting for transfers between devices, local(): lax.all_to_all(basis.reshape(col_count, per_leaf * slab, probes), 'col',...  19.4 us
  transfers between devices with their start and end apart: 25, of which 10 were waited for; matrix products, arithmetic and copies ran while one was open for 10% of the time, Pallas kernels for 19%

profile of v2, /device:TPU:0, one launch (start us, length us, event | category | flops | bytes accessed | tf_op | source)
XLA Modules:
  0.0 476.0 jit_solution(10022830123122143769)
XLA Ops:
  7.2 5.7 %copy.112.test_ref = bf16[2,1792,448]{2,1,0:T(8,128)(2,1)} copy(bf16[2,1792,448]{1,2,0:T(8,128)(2,1)} %param.8) | data formatting | bytes 6422528 | tf_op args[3]
  13.0 2.0 copy-done.1
  15.0 10.5 %probe.6 = (f32[28,4,16,448]{3,2,1,0:T(8,128)S(1)}, f32[28,4,16,448]{3,2,1,0:T(8,128)S(1)}) custom-call(s32[1]{0:T(128)} %bitcast.parity_ref, bf16[2,3584,1792]{2,1,0:T(8,128)(2,1)} %front_ref.3, bf16[2,1792,448]{2,1,0:T(8,128)(2,1)S(1)} %copy-done.1), custom_call_target="tpu_custom_call" | custom-call | flops 5754585088 | bytes 20873216 | tf_op jit(solution)/shard_map/probe/pallas_call | solution.py:114
  25.6 2.9 copy.114
  28.9 12.0 %probe.7 = (f32[28,4,16,448]{3,2,1,0:T(8,128)S(1)}, f32[28,4,16,448]{3,2,1,0:T(8,128)}) custom-call(s32[1]{0:T(128)} %bitcast.parity_ref, bf16[2,3584,1792]{2,1,0:T(8,128)(2,1)} %front_ref.3, bf16[2,1792,448]{2,1,0:T(8,128)(2,1)S(1)} %copy-done.1), custom_call_target="tpu_custom_call" | custom-call | flops 5754585088 | bytes 20873216 | tf_op jit(solution)/shard_map/probe/pallas_call | solution.py:114
  40.9 1.9 copy-done.2
  42.9 3.2 fusion.39
  46.1 4.1 collective-permute-start.10
  50.2 1.3 collective-permute-start.11
  52.2 2.8 fusion.45
  55.0 1.6 collective-permute-start.13
  56.6 2.1 collective-permute-start.14
  58.7 2.1 fusion.42
  60.8 11.2 %collective-permute-done.10 = bf16[28,16,448]{2,1,0:T(8,128)(2,1)S(1)} collective-permute-done((bf16[28,16,448]{2,1,0:T(8,128)(2,1)S(1)}, bf16[28,16,448]{2,1,0:T(8,128)(2,1)S(1)}, u32[]{:S(2)}, u32[]{:S(2)}) %collective-permute-start.10) | collective-permute-done | bytes 401440 | tf_op jit(solution)/shard_map/ppermute | solution.py:150
  72.0 12.2 %collective-permute-start.15 = (bf16[28,16,448]{2,1,0:T(8,128)(2,1)}, bf16[28,16,448]{2,1,0:T(8,128)(2,1)}, u32[]{:S(2)}, u32[]{:S(2)}) collective-permute-start(bf16[28,16,448]{2,1,0:T(8,128)(2,1)} %fusion.42), channel_id=1, source_target_pairs={{0,6},{1,7},{2,0},{3,1},{4,2},{5,3},{6,4},{7,5},{8,14},{9,15},{10,... | collective-permute-start | bytes 1204232 | tf_op jit(solution)/shard_map/ppermute | solution.py:150
  84.2 1.8 fusion.31
  86.1 6.5 %collective-permute-done.13 = bf16[28,16,448]{2,1,0:T(8,128)(2,1)S(1)} collective-permute-done((bf16[28,16,448]{2,1,0:T(8,128)(2,1)}, bf16[28,16,448]{2,1,0:T(8,128)(2,1)S(1)}, u32[]{:S(2)}, u32[]{:S(2)}) %collective-permute-start.13) | collective-permute-done | bytes 401440 | tf_op jit(solution)/shard_map/ppermute | solution.py:150
  92.6 28.0 %collective-permute-done.14 = bf16[28,16,448]{2,1,0:T(8,128)(2,1)S(1)} collective-permute-done((bf16[28,16,448]{2,1,0:T(8,128)(2,1)}, bf16[28,16,448]{2,1,0:T(8,128)(2,1)S(1)}, u32[]{:S(2)}, u32[]{:S(2)}) %collective-permute-start.14) | collective-permute-done | bytes 401440 | tf_op jit(solution)/shard_map/ppermute | solution.py:150
  120.6 2.0 fusion.22
  122.6 1.4 pad_maximum_fusion
  124.1 1.1 copy-done.9
  125.1 3.7 copy.100
  128.8 2.0 copy-done
  130.8 17.1 %probe.4 = (f32[28,4,16,448]{3,2,1,0:T(8,128)S(1)}, f32[28,4,16,448]{3,2,1,0:T(8,128)S(1)}) custom-call(s32[1]{0:T(128)} %bitcast.parity_ref, bf16[1,7168,3584]{2,1,0:T(8,128)(2,1)} %bitcast.135, bf16[1,3584,448]{2,1,0:T(8,128)(2,1)S(1)} %bitcast.130), custom_call_target="tpu_custom_call" | custom-call | flops 11509170176 | bytes 35323904 | tf_op jit(solution)/shard_map/probe/pallas_call | solution.py:114
  148.0 3.2 copy.102
  151.2 17.8 %probe.5 = (f32[28,4,16,448]{3,2,1,0:T(8,128)S(1)}, f32[28,4,16,448]{3,2,1,0:T(8,128)}) custom-call(s32[1]{0:T(128)} %bitcast.parity_ref, bf16[1,7168,3584]{2,1,0:T(8,128)(2,1)} %bitcast.136, bf16[1,3584,448]{2,1,0:T(8,128)(2,1)S(1)} %bitcast.131), custom_call_target="tpu_custom_call" | custom-call | flops 11509170176 | bytes 35323904 | tf_op jit(solution)/shard_map/probe/pallas_call | solution.py:114
  169.0 1.9 copy-done.5
  171.4 4.1 fusion.35
  175.5 9.5 %collective-permute-start.1 = (bf16[28,16,448]{2,1,0:T(8,128)(2,1)S(1)}, bf16[28,16,448]{2,1,0:T(8,128)(2,1)S(1)}, u32[]{:S(2)}, u32[]{:S(2)}) collective-permute-start(bf16[28,16,448]{2,1,0:T(8,128)(2,1)S(1)} %get-tuple-element.31), channel_id=1, source_target_pairs={{0,2},{1,3},{2,4},{3,5},{4,6},{5,7},{6,0},{7,1},{8,10},{9,11},{10,... | collective-permute-start | bytes 1204232 | tf_op jit(solution)/shard_map/ppermute | solution.py:150
  185.0 4.0 collective-permute-start.2
  189.1 1.8 fusion.43
  190.9 2.1 collective-permute-start.5
  192.9 1.1 collective-permute-start.6
  194.0 1.3 fusion.38
  195.4 4.6 collective-permute-done.1
  200.0 3.2 collective-permute-start.7
  203.2 16.5 %collective-permute-done.2 = bf16[28,16,448]{2,1,0:T(8,128)(2,1)S(1)} collective-permute-done((bf16[28,16,448]{2,1,0:T(8,128)(2,1)S(1)}, bf16[28,16,448]{2,1,0:T(8,128)(2,1)S(1)}, u32[]{:S(2)}, u32[]{:S(2)}) %collective-permute-start.2) | collective-permute-done | bytes 401440 | tf_op jit(solution)/shard_map/ppermute | solution.py:150
  219.7 1.8 fusion.33
  221.5 8.0 %collective-permute-done.5 = bf16[28,16,448]{2,1,0:T(8,128)(2,1)S(1)} collective-permute-done((bf16[28,16,448]{2,1,0:T(8,128)(2,1)S(1)}, bf16[28,16,448]{2,1,0:T(8,128)(2,1)S(1)}, u32[]{:S(2)}, u32[]{:S(2)}) %collective-permute-start.5) | collective-permute-done | bytes 401440 | tf_op jit(solution)/shard_map/ppermute | solution.py:150
  229.5 28.9 %collective-permute-done.6 = bf16[28,16,448]{2,1,0:T(8,128)(2,1)S(1)} collective-permute-done((bf16[28,16,448]{2,1,0:T(8,128)(2,1)S(1)}, bf16[28,16,448]{2,1,0:T(8,128)(2,1)S(1)}, u32[]{:S(2)}, u32[]{:S(2)}) %collective-permute-start.6) | collective-permute-done | bytes 401440 | tf_op jit(solution)/shard_map/ppermute | solution.py:150
  258.5 2.5 fusion.28
  261.0 9.9 %fusion.9 = f32[56,16,448]{2,0,1:T(8,128)S(1)} fusion(f32[2,112,16,448]{3,2,1,0:T(8,128)} %all-gather.2.cloned.1.call-done, s32[2,112]{1,0:T(2,128)S(1)} %broadcast_subtract_fusion), kind=kOutput, calls=%fused_computation.12 | convolution fusion | flops 1078997248 | bytes 8029056 | tf_op jit(solution)/shard_map/cpn,cnsr->psr/dot_general | solution.py:224
  270.9 1.2 maximum_add_fusion
  272.1 1.8 copy.127
  273.8 11.6 %all-to-all-start = ((f32[8,112,448]{1,2,0:T(8,128)}), f32[8,112,448]{1,2,0:T(8,128)S(1)}, u32[]{:S(2)}, u32[]{:S(2)}) async-start(f32[8,112,448]{1,2,0:T(8,128)} %copy.127), calls=%async_computation | async-start | bytes 3670016 | tf_op jit(solution)/shard_map/all_to_all | solution.py:228
  285.4 3.9 constant_dynamic-slice_fusion
  289.4 5.0 %collective-permute-start.17 = (bf16[896,896]{1,0:T(8,128)(2,1)}, bf16[896,896]{1,0:T(8,128)(2,1)}, u32[]{:S(2)}, u32[]{:S(2)}) collective-permute-start(bf16[896,896]{1,0:T(8,128)(2,1)} %get-tuple-element.23), channel_id=1, source_target_pairs={{0,3},{1,7},{10,11},{11,15},{20,19},{21,23},{30,27},{31,31}} | collective-permute-start | bytes 4816904 | tf_op jit(solution)/shard_map/ppermute | solution.py:199
  294.4 4.8 %collective-permute-start.19 = (bf16[896,896]{1,0:T(8,128)(2,1)}, bf16[896,896]{1,0:T(8,128)(2,1)}, u32[]{:S(2)}, u32[]{:S(2)}) collective-permute-start(bf16[896,896]{1,0:T(8,128)(2,1)} %get-tuple-element.22), channel_id=1, source_target_pairs={{0,1},{1,5},{10,9},{11,13},{20,17},{21,21},{30,25},{31,29}} | collective-permute-start | bytes 4816904 | tf_op jit(solution)/shard_map/ppermute | solution.py:199
  299.2 29.7 %all-to-all-done = f32[8,112,448]{1,2,0:T(8,128)S(1)} async-done(((f32[8,112,448]{1,2,0:T(8,128)}), f32[8,112,448]{1,2,0:T(8,128)S(1)}, u32[]{:S(2)}, u32[]{:S(2)}) %all-to-all-start) | async-done | bytes 1605664 | tf_op jit(solution)/shard_map/all_to_all | solution.py:228
  328.9 2.3 copy.128
  331.2 1.9 reshape.59
  333.1 4.0 constant_dynamic-slice_fusion.3
  337.0 11.5 %collective-permute-start.16 = (bf16[896,896]{1,0:T(8,128)(2,1)}, bf16[896,896]{1,0:T(8,128)(2,1)}, u32[]{:S(2)}, u32[]{:S(2)}) collective-permute-start(bf16[896,896]{1,0:T(8,128)(2,1)} %get-tuple-element.25), channel_id=1, source_target_pairs={{0,2},{1,6},{10,10},{11,14},{20,18},{21,22},{30,26},{31,30}} | collective-permute-start | bytes 4816904 | tf_op jit(solution)/shard_map/ppermute | solution.py:199
  348.5 13.8 %collective-permute-start.18 = (bf16[896,896]{1,0:T(8,128)(2,1)}, bf16[896,896]{1,0:T(8,128)(2,1)}, u32[]{:S(2)}, u32[]{:S(2)}) collective-permute-start(bf16[896,896]{1,0:T(8,128)(2,1)} %get-tuple-element.24), channel_id=1, source_target_pairs={{0,0},{1,4},{10,8},{11,12},{20,16},{21,20},{30,24},{31,28}} | collective-permute-start | bytes 4816904 | tf_op jit(solution)/shard_map/ppermute | solution.py:199
  362.4 42.2 %leaf_basis.1 = bf16[448,896]{1,0:T(8,128)(2,1)S(1)} custom-call(f32[448,896]{1,0:T(8,128)S(1)} %bitcast.134), custom_call_target="tpu_custom_call" | custom-call | flops 7193231360 | bytes 2408448 | tf_op jit(solution)/shard_map/leaf_basis/pallas_call | solution.py:79
  406.3 1.0 reshape.60
  407.3 1.1 copy.129
  408.4 3.6 all-to-all-start.1
  412.0 4.2 convolution_multiply_fusion
  416.3 19.4 %all-to-all-done.1 = bf16[8,112,448]{1,2,0:T(8,128)(2,1)S(1)} async-done(((bf16[8,112,448]{1,2,0:T(8,128)(2,1)}), bf16[8,112,448]{1,2,0:T(8,128)(2,1)S(1)}, u32[]{:S(2)}, u32[]{:S(2)}) %all-to-all-start.1) | async-done | bytes 802848 | tf_op jit(solution)/shard_map/all_to_all | solution.py:240
  435.6 8.9 %all-to-all-start.2 = ((f32[8,56,448]{2,1,0:T(8,128)}), f32[8,56,448]{2,1,0:T(8,128)S(1)}, u32[]{:S(2)}, u32[]{:S(2)}) async-start(f32[8,56,448]{2,1,0:T(8,128)} %bitcast.31), calls=%async_computation.2 | async-start | bytes 1835008 | tf_op jit(solution)/shard_map/all_to_all | solution.py:261
  444.5 1.3 copy.130
  445.8 22.5 %all-to-all-done.2 = f32[8,56,448]{2,1,0:T(8,128)S(1)} async-done(((f32[8,56,448]{2,1,0:T(8,128)}), f32[8,56,448]{2,1,0:T(8,128)S(1)}, u32[]{:S(2)}, u32[]{:S(2)}) %all-to-all-start.2) | async-done | bytes 802848 | tf_op jit(solution)/shard_map/all_to_all | solution.py:261
  468.3 0.9 copy.163
  (45 shorter events, 3.5 us)
Async XLA Ops:
  7.2 253.8 %all-gather.2.cloned.1.call-start = ((), (), s32[]{:S(2)}) async-start(), calls=%async_computation.3 | async-start | bytes 9175040 | tf_op jit(solution)/shard_map/all_gather | solution.py:218
  13.0 2.0 copy-start.1
  25.5 2.9 copy-start.4
  28.5 14.4 %collective-permute-start.8 = (f32[28,4,16,448]{3,2,0,1:T(8,128)}, f32[28,4,16,448]{3,2,0,1:T(8,128)}, u32[]{:S(2)}, u32[]{:S(2)}) collective-permute-start(f32[28,4,16,448]{3,2,0,1:T(8,128)} %copy.114), channel_id=1, source_target_pairs={{0,1},{1,0},{2,3},{3,2},{4,5},{5,4},{6,7},{7,6},{8,9},{9,8},{10,11... | collective-permute-start | bytes 9633800 | tf_op jit(solution)/shard_map/ppermute | solution.py:138
  40.9 1.9 copy-start.2
  42.8 9.4 %collective-permute-start.12 = (f32[28,4,16,448]{3,2,1,0:T(8,128)}, f32[28,4,16,448]{3,2,1,0:T(8,128)}, u32[]{:S(2)}, u32[]{:S(2)}) collective-permute-start(f32[28,4,16,448]{3,2,1,0:T(8,128)} %get-tuple-element.19), channel_id=1, source_target_pairs={{0,1},{1,0},{2,3},{3,2},{4,5},{5,4},{6,7},{7,6},{8,9},{9,8},{10,11... | collective-permute-start | bytes 9633800 | tf_op jit(solution)/shard_map/ppermute | solution.py:138
  42.8 9.4 %copy-start.3 = (f32[28,4,16,448]{3,2,1,0:T(8,128)S(1)}, f32[28,4,16,448]{3,2,1,0:T(8,128)}, u32[]{:S(2)}) copy-start(f32[28,4,16,448]{3,2,1,0:T(8,128)} %copy-done.2) | copy-start | bytes 9633796
  46.1 25.9 %collective-permute-start.10 = (bf16[28,16,448]{2,1,0:T(8,128)(2,1)S(1)}, bf16[28,16,448]{2,1,0:T(8,128)(2,1)S(1)}, u32[]{:S(2)}, u32[]{:S(2)}) collective-permute-start(bf16[28,16,448]{2,1,0:T(8,128)(2,1)S(1)} %get-tuple-element.28), channel_id=1, source_target_pairs={{0,4},{1,5},{2,6},{3,7},{4,0},{5,1},{6,2},{7,3},{8,12},{9,13},{10,... | collective-permute-start | bytes 1204232 | tf_op jit(solution)/shard_map/ppermute | solution.py:150
  50.2 34.0 %collective-permute-start.11 = (bf16[28,16,448]{2,1,0:T(8,128)(2,1)S(1)}, bf16[28,16,448]{2,1,0:T(8,128)(2,1)S(1)}, u32[]{:S(2)}, u32[]{:S(2)}) collective-permute-start(bf16[28,16,448]{2,1,0:T(8,128)(2,1)S(1)} %get-tuple-element.27), channel_id=1, source_target_pairs={{0,6},{1,7},{2,0},{3,1},{4,2},{5,3},{6,4},{7,5},{8,14},{9,15},{10,... | collective-permute-start | bytes 1204232 | tf_op jit(solution)/shard_map/ppermute | solution.py:150
  51.6 32.7 %collective-permute-start.9 = (bf16[28,16,448]{2,1,0:T(8,128)(2,1)S(1)}, bf16[28,16,448]{2,1,0:T(8,128)(2,1)S(1)}, u32[]{:S(2)}, u32[]{:S(2)}) collective-permute-start(bf16[28,16,448]{2,1,0:T(8,128)(2,1)S(1)} %get-tuple-element.26), channel_id=1, source_target_pairs={{0,2},{1,3},{2,4},{3,5},{4,6},{5,7},{6,0},{7,1},{8,10},{9,11},{10,... | collective-permute-start | bytes 1204232 | tf_op jit(solution)/shard_map/ppermute | solution.py:150
  55.0 37.6 %collective-permute-start.13 = (bf16[28,16,448]{2,1,0:T(8,128)(2,1)}, bf16[28,16,448]{2,1,0:T(8,128)(2,1)S(1)}, u32[]{:S(2)}, u32[]{:S(2)}) collective-permute-start(bf16[28,16,448]{2,1,0:T(8,128)(2,1)} %get-tuple-element.29), channel_id=1, source_target_pairs={{0,2},{1,3},{2,4},{3,5},{4,6},{5,7},{6,0},{7,1},{8,10},{9,11},{10,... | collective-permute-start | bytes 1204232 | tf_op jit(solution)/shard_map/ppermute | solution.py:150
  56.6 64.0 %collective-permute-start.14 = (bf16[28,16,448]{2,1,0:T(8,128)(2,1)}, bf16[28,16,448]{2,1,0:T(8,128)(2,1)S(1)}, u32[]{:S(2)}, u32[]{:S(2)}) collective-permute-start(bf16[28,16,448]{2,1,0:T(8,128)(2,1)} %get-tuple-element.30), channel_id=1, source_target_pairs={{0,4},{1,5},{2,6},{3,7},{4,0},{5,1},{6,2},{7,3},{8,12},{9,13},{10,... | collective-permute-start | bytes 1204232 | tf_op jit(solution)/shard_map/ppermute | solution.py:150
  72.0 48.6 %collective-permute-start.15 = (bf16[28,16,448]{2,1,0:T(8,128)(2,1)}, bf16[28,16,448]{2,1,0:T(8,128)(2,1)}, u32[]{:S(2)}, u32[]{:S(2)}) collective-permute-start(bf16[28,16,448]{2,1,0:T(8,128)(2,1)} %fusion.42), channel_id=1, source_target_pairs={{0,6},{1,7},{2,0},{3,1},{4,2},{5,3},{6,4},{7,5},{8,14},{9,15},{10,... | collective-permute-start | bytes 1204232 | tf_op jit(solution)/shard_map/ppermute | solution.py:150
  122.6 2.6 copy-start.9
  128.8 2.0 copy-start
  148.0 3.2 copy-start.7
  151.2 20.2 %collective-permute-start = (f32[28,4,16,448]{3,2,0,1:T(8,128)}, f32[28,4,16,448]{3,2,0,1:T(8,128)}, u32[]{:S(2)}, u32[]{:S(2)}) collective-permute-start(f32[28,4,16,448]{3,2,0,1:T(8,128)} %copy.102), channel_id=1, source_target_pairs={{0,1},{1,0},{2,3},{3,2},{4,5},{5,4},{6,7},{7,6},{8,9},{9,8},{10,11... | collective-permute-start | bytes 9633800 | tf_op jit(solution)/shard_map/ppermute | solution.py:138
  169.0 1.9 copy-start.5
  170.9 18.2 %collective-permute-start.4 = (f32[28,4,16,448]{3,2,1,0:T(8,128)}, f32[28,4,16,448]{3,2,1,0:T(8,128)}, u32[]{:S(2)}, u32[]{:S(2)}) collective-permute-start(f32[28,4,16,448]{3,2,1,0:T(8,128)} %get-tuple-element.15), channel_id=1, source_target_pairs={{0,1},{1,0},{2,3},{3,2},{4,5},{5,4},{6,7},{7,6},{8,9},{9,8},{10,11... | collective-permute-start | bytes 9633800 | tf_op jit(solution)/shard_map/ppermute | solution.py:138
  171.4 17.7 %copy-start.6 = (f32[28,4,16,448]{3,2,1,0:T(8,128)S(1)}, f32[28,4,16,448]{3,2,1,0:T(8,128)}, u32[]{:S(2)}) copy-start(f32[28,4,16,448]{3,2,1,0:T(8,128)} %copy-done.5) | copy-start | bytes 9633796
  175.5 27.6 %copy-start.10 = (s32[2,112]{1,0:T(2,128)S(1)}, s32[2,112]{1,0:T(2,128)}, u32[]{:S(2)}) copy-start(s32[2,112]{1,0:T(2,128)} %param.9) | copy-start | bytes 2692
  175.5 24.5 %collective-permute-start.1 = (bf16[28,16,448]{2,1,0:T(8,128)(2,1)S(1)}, bf16[28,16,448]{2,1,0:T(8,128)(2,1)S(1)}, u32[]{:S(2)}, u32[]{:S(2)}) collective-permute-start(bf16[28,16,448]{2,1,0:T(8,128)(2,1)S(1)} %get-tuple-element.31), channel_id=1, source_target_pairs={{0,2},{1,3},{2,4},{3,5},{4,6},{5,7},{6,0},{7,1},{8,10},{9,11},{10,... | collective-permute-start | bytes 1204232 | tf_op jit(solution)/shard_map/ppermute | solution.py:150
  185.0 34.6 %collective-permute-start.2 = (bf16[28,16,448]{2,1,0:T(8,128)(2,1)S(1)}, bf16[28,16,448]{2,1,0:T(8,128)(2,1)S(1)}, u32[]{:S(2)}, u32[]{:S(2)}) collective-permute-start(bf16[28,16,448]{2,1,0:T(8,128)(2,1)S(1)} %get-tuple-element.33), channel_id=1, source_target_pairs={{0,4},{1,5},{2,6},{3,7},{4,0},{5,1},{6,2},{7,3},{8,12},{9,13},{10,... | collective-permute-start | bytes 1204232 | tf_op jit(solution)/shard_map/ppermute | solution.py:150
  189.0 30.6 %collective-permute-start.3 = (bf16[28,16,448]{2,1,0:T(8,128)(2,1)S(1)}, bf16[28,16,448]{2,1,0:T(8,128)(2,1)S(1)}, u32[]{:S(2)}, u32[]{:S(2)}) collective-permute-start(bf16[28,16,448]{2,1,0:T(8,128)(2,1)S(1)} %get-tuple-element.32), channel_id=1, source_target_pairs={{0,6},{1,7},{2,0},{3,1},{4,2},{5,3},{6,4},{7,5},{8,14},{9,15},{10,... | collective-permute-start | bytes 1204232 | tf_op jit(solution)/shard_map/ppermute | solution.py:150
  190.9 38.6 %collective-permute-start.5 = (bf16[28,16,448]{2,1,0:T(8,128)(2,1)S(1)}, bf16[28,16,448]{2,1,0:T(8,128)(2,1)S(1)}, u32[]{:S(2)}, u32[]{:S(2)}) collective-permute-start(bf16[28,16,448]{2,1,0:T(8,128)(2,1)S(1)} %get-tuple-element.34), channel_id=1, source_target_pairs={{0,2},{1,3},{2,4},{3,5},{4,6},{5,7},{6,0},{7,1},{8,10},{9,11},{10,... | collective-permute-start | bytes 1204232 | tf_op jit(solution)/shard_map/ppermute | solution.py:150
  192.9 65.5 %collective-permute-start.6 = (bf16[28,16,448]{2,1,0:T(8,128)(2,1)S(1)}, bf16[28,16,448]{2,1,0:T(8,128)(2,1)S(1)}, u32[]{:S(2)}, u32[]{:S(2)}) collective-permute-start(bf16[28,16,448]{2,1,0:T(8,128)(2,1)S(1)} %get-tuple-element.35), channel_id=1, source_target_pairs={{0,4},{1,5},{2,6},{3,7},{4,0},{5,1},{6,2},{7,3},{8,12},{9,13},{10,... | collective-permute-start | bytes 1204232 | tf_op jit(solution)/shard_map/ppermute | solution.py:150
  200.0 58.5 %collective-permute-start.7 = (bf16[28,16,448]{2,1,0:T(8,128)(2,1)S(1)}, bf16[28,16,448]{2,1,0:T(8,128)(2,1)S(1)}, u32[]{:S(2)}, u32[]{:S(2)}) collective-permute-start(bf16[28,16,448]{2,1,0:T(8,128)(2,1)S(1)} %fusion.38), channel_id=1, source_target_pairs={{0,6},{1,7},{2,0},{3,1},{4,2},{5,3},{6,4},{7,5},{8,14},{9,15},{10,... | collective-permute-start | bytes 1204232 | tf_op jit(solution)/shard_map/ppermute | solution.py:150
  261.0 9.9 %copy-start.8 = (f32[28,16,448]{2,1,0:T(8,128)S(1)}, f32[28,16,448]{2,1,0:T(8,128)}, u32[]{:S(2)}) copy-start(f32[28,16,448]{2,1,0:T(8,128)} %fusion.28) | copy-start | bytes 2408452
  273.8 55.0 %all-to-all-start = ((f32[8,112,448]{1,2,0:T(8,128)}), f32[8,112,448]{1,2,0:T(8,128)S(1)}, u32[]{:S(2)}, u32[]{:S(2)}) async-start(f32[8,112,448]{1,2,0:T(8,128)} %copy.127), calls=%async_computation | async-start | bytes 3670016 | tf_op jit(solution)/shard_map/all_to_all | solution.py:228
  289.4 122.6 %collective-permute-start.17 = (bf16[896,896]{1,0:T(8,128)(2,1)}, bf16[896,896]{1,0:T(8,128)(2,1)}, u32[]{:S(2)}, u32[]{:S(2)}) collective-permute-start(bf16[896,896]{1,0:T(8,128)(2,1)} %get-tuple-element.23), channel_id=1, source_target_pairs={{0,3},{1,7},{10,11},{11,15},{20,19},{21,23},{30,27},{31,31}} | collective-permute-start | bytes 4816904 | tf_op jit(solution)/shard_map/ppermute | solution.py:199
  294.4 117.6 %collective-permute-start.19 = (bf16[896,896]{1,0:T(8,128)(2,1)}, bf16[896,896]{1,0:T(8,128)(2,1)}, u32[]{:S(2)}, u32[]{:S(2)}) collective-permute-start(bf16[896,896]{1,0:T(8,128)(2,1)} %get-tuple-element.22), channel_id=1, source_target_pairs={{0,1},{1,5},{10,9},{11,13},{20,17},{21,21},{30,25},{31,29}} | collective-permute-start | bytes 4816904 | tf_op jit(solution)/shard_map/ppermute | solution.py:199
  337.0 75.0 %collective-permute-start.16 = (bf16[896,896]{1,0:T(8,128)(2,1)}, bf16[896,896]{1,0:T(8,128)(2,1)}, u32[]{:S(2)}, u32[]{:S(2)}) collective-permute-start(bf16[896,896]{1,0:T(8,128)(2,1)} %get-tuple-element.25), channel_id=1, source_target_pairs={{0,2},{1,6},{10,10},{11,14},{20,18},{21,22},{30,26},{31,30}} | collective-permute-start | bytes 4816904 | tf_op jit(solution)/shard_map/ppermute | solution.py:199
  348.5 63.5 %collective-permute-start.18 = (bf16[896,896]{1,0:T(8,128)(2,1)}, bf16[896,896]{1,0:T(8,128)(2,1)}, u32[]{:S(2)}, u32[]{:S(2)}) collective-permute-start(bf16[896,896]{1,0:T(8,128)(2,1)} %get-tuple-element.24), channel_id=1, source_target_pairs={{0,0},{1,4},{10,8},{11,12},{20,16},{21,20},{30,24},{31,28}} | collective-permute-start | bytes 4816904 | tf_op jit(solution)/shard_map/ppermute | solution.py:199
  406.2 5.8 %collective-permute-start.20 = (bf16[896,448]{0,1:T(8,128)(2,1)S(1)}, bf16[896,448]{0,1:T(8,128)(2,1)}, u32[]{:S(2)}, u32[]{:S(2)}) collective-permute-start(bf16[896,448]{0,1:T(8,128)(2,1)S(1)} %copy.133), channel_id=1, source_target_pairs={{0,1},{1,0},{2,3},{3,2},{4,5},{5,4},{6,7},{7,6},{8,9},{9,8},{10,11... | collective-permute-start | bytes 2408456 | tf_op jit(solution)/shard_map/ppermute | solution.py:250
  408.4 27.2 %all-to-all-start.1 = ((bf16[8,112,448]{1,2,0:T(8,128)(2,1)}), bf16[8,112,448]{1,2,0:T(8,128)(2,1)S(1)}, u32[]{:S(2)}, u32[]{:S(2)}) async-start(bf16[8,112,448]{1,2,0:T(8,128)(2,1)} %copy.129), calls=%async_computation.1 | async-start | bytes 1835008 | tf_op jit(solution)/shard_map/all_to_all | solution.py:240
  435.6 32.6 %all-to-all-start.2 = ((f32[8,56,448]{2,1,0:T(8,128)}), f32[8,56,448]{2,1,0:T(8,128)S(1)}, u32[]{:S(2)}, u32[]{:S(2)}) async-start(f32[8,56,448]{2,1,0:T(8,128)} %bitcast.31), calls=%async_computation.2 | async-start | bytes 1835008 | tf_op jit(solution)/shard_map/all_to_all | solution.py:261
Sparse Core Ops, SparseCore 0:
  124.2 89.0 all-gather.1
